TPU v7x, 32 devices: a whole 2x2x4 slice. The times are simulated.
32 devices in a mesh: field: 16 (over z, y, core), probe: 2 (over x).
Axes of the slice: x: 2, y: 2, z: 4, core: 2. Of those that a mesh axis runs over, the one named last changes fastest.
Arguments:
- probes: bfloat16 [16, 4, 512, 256], P('probe', None, 'field'), may hold values from -6 to 6
- matern_shift: float32 [4, 512, 256], P(None, 'field'), may hold values from 0.25 to 2
- diffusivity: float32 [4, 512, 256], P(None, 'field'), may hold values from 0.03 to 0.1
- sensor_count: int32 [16], P('field'), may hold values from 1 to 256, 2560 in all
- sensor_cell: int32 [16, 256], P('field'), may hold values from 0 to 32767
- sensor_owner: int32 [16, 256, 1], P('field'), may hold values from 0 to 15; in each aligned block of 256 rows (0 to 255, 256 to 511, ..., all dimensions but the last counted through in order) at most 24 rows name the same one
- design_logit: float32 [16, 16, 24], P('field'), may hold values from -6 to 6
- noise_precision: float32 [16, 16, 24], P('field'), may hold values from 1 to 8
Outputs:
- hessian_probes: float32 [16, 4, 512, 256], P('probe', None, 'field')
- tiles: float32 [16, 16], P('probe')
- weight_grad: float32 [16, 16, 24], P('field')
Inputs may be any that keep to these rules, and one draw needn't show every extreme that they name: `sensor_count`: the counts sum to 2560 and the largest is 256. `sensor_cell`: flat cell index within the block; several slots may share a cell. `sensor_owner`: among the 256 slots of one block, live or not, no owner is named by more than 24 slots, a bound that some block reaches.
All inputs are finite; a program needn't handle non-finite values. No bound on the sum of `sensor_count` on one device may be relied on, other than what follows from the above.
Results may differ from a plain program's by a relative error of at most 0.00035.
Values may be sent and summed in bfloat16 or wider, within the bound.
A program may use at most 128 MiB of HBM per device.

v0:
```python
import math
import jax
import jax.numpy as jnp
from jax import lax
from jax.sharding import PartitionSpec as P

SWEEPS = 4
STEPS = 6
SENS_DEV = 160
advect_speed = 0.3


def with_halo(value, sides, width):
    for axis, dim in sides:
        size, length = (lax.axis_size(axis), value.shape[dim])
        up = [(i, (i + 1) % size) for i in range(size)]
        down = [(j, i) for i, j in up]
        last = lax.slice_in_dim(value, length - width, length, axis=dim)
        first = lax.slice_in_dim(value, 0, width, axis=dim)
        before = lax.ppermute(last, axis, up)
        after = lax.ppermute(first, axis, down)
        value = jnp.concatenate([before, value, after], axis=dim)
    return value


def neighbours(extended):
    middle = extended[:, :, 1:-1]
    west_cells = extended[:, :, :-2]
    east_cells = extended[:, :, 2:]
    side_pad = jnp.pad(middle, ((0, 0), (0, 0), (0, 0), (1, 1)))
    depth_pad = jnp.pad(middle, ((0, 0), (1, 1), (0, 0), (0, 0)))
    beside_all = (
        west_cells
        + east_cells
        + (side_pad[..., :-2] + side_pad[..., 2:])
        + (depth_pad[:, :-2] + depth_pad[:, 2:])
    )
    return (middle, west_cells, east_cells, beside_all)


def prior_apply(source, diagonal):
    state = source / diagonal
    for sweep in range(SWEEPS):
        extended = with_halo(state, (("field", 2),), 1)
        middle, west_cells, east_cells, beside_all = neighbours(extended)
        state = (source + beside_all) / diagonal
    return state


def on_device(
    probes,
    matern_shift,
    diffusivity,
    sensor_count,
    sensor_cell,
    sensor_owner,
    design_logit,
    noise_precision,
):
    probe_count = probes.shape[0]
    block_cx = probes.shape[2]
    cell_count = probes.shape[1] * probes.shape[2] * probes.shape[3]
    field_count = lax.axis_size("field")
    slot_cap = design_logit.shape[2]
    slot_count = sensor_cell.shape[1]
    diagonal = matern_shift + 6.0
    depth = 2
    coef_wide = with_halo(diffusivity, (("field", 1),), depth)
    state = prior_apply(probes.astype(jnp.float32), diagonal)
    for rounds in range(STEPS // depth):
        extended = with_halo(state, (("field", 2),), depth)
        for inner in range(depth):
            width = block_cx + 2 * (depth - inner - 1)
            coef_mid = coef_wide[:, inner + 1 : inner + 1 + width]
            middle, west_cells, east_cells, beside_all = neighbours(extended)
            extended = (
                middle
                + coef_mid * (beside_all - 6.0 * middle)
                - advect_speed * (middle - west_cells)
            )
        state = extended
    slots = jnp.arange(slot_count, dtype=jnp.int32)
    live = (slots < sensor_count[0]).astype(jnp.float32)
    cells = sensor_cell[0]
    owner = sensor_owner[0, :, 0]
    same = owner[:, None] == owner[None, :]
    earlier = slots[None, :] < slots[:, None]
    position = jnp.sum(jnp.logical_and(same, earlier), axis=1)
    target = owner * slot_cap + position
    table = (
        jnp.arange(field_count * slot_cap, dtype=jnp.int32)[:, None] == target[None, :]
    ).astype(jnp.float32)
    flat_state = state.reshape(probe_count, cell_count)
    observed = jnp.take(flat_state, cells, axis=1) * live[None, :]
    outgoing = lax.dot_general(
        table, observed, (((1,), (1,)), ((), ())), precision=lax.Precision.HIGHEST
    )
    outgoing = outgoing.reshape(field_count, slot_cap, probe_count)
    received = lax.all_to_all(outgoing, "field", split_axis=0, concat_axis=0, tiled=True)
    gated = jax.nn.sigmoid(design_logit[0])
    weight_slot = gated * noise_precision[0]
    weighted = received * weight_slot[:, :, None]
    returned = lax.all_to_all(weighted, "field", split_axis=0, concat_axis=0, tiled=True)
    per_sensor = lax.dot_general(
        table,
        returned.reshape(field_count * slot_cap, probe_count),
        (((0,), (0,)), ((), ())),
        precision=lax.Precision.HIGHEST,
    )
    injected = jnp.zeros((probe_count, cell_count), jnp.float32).at[:, cells].add(per_sensor.T)
    adjoint = injected.reshape(probes.shape)
    for rounds in range(STEPS // depth):
        extended = with_halo(adjoint, (("field", 2),), depth)
        for inner in range(depth):
            width = block_cx + 2 * (depth - inner)
            scaled = coef_wide[:, inner : inner + width] * extended
            scaled_mid, scaled_west, scaled_east, scaled_around = neighbours(scaled)
            middle = extended[:, :, 1:-1]
            east_cells = extended[:, :, 2:]
            extended = (
                middle + (scaled_around - 6.0 * scaled_mid) - advect_speed * (middle - east_cells)
            )
        adjoint = extended
    hessian_probes = prior_apply(adjoint, diagonal)
    flat_result = hessian_probes.reshape(probe_count, cell_count)
    piece = lax.all_gather(probes, "probe", axis=0, tiled=True)
    flat_piece = piece.reshape(piece.shape[0], cell_count).astype(jnp.float32)
    columns = lax.dot_general(
        flat_result, flat_piece, (((1,), (1,)), ((), ())), precision=lax.Precision.HIGHEST
    )
    scale_factor = 1.0 / math.sqrt(SENS_DEV * field_count)
    tiles = lax.psum(columns, "field") * scale_factor
    squares = jnp.sum(received * received, axis=2)
    total_squares = lax.psum(squares, "probe")
    weight_grad = gated * (1.0 - gated) * noise_precision[0] * total_squares
    return (hessian_probes, tiles, weight_grad[None])


def solution(mesh):
    in_specs = (
        P("probe", None, "field", None),
        P(None, "field", None),
        P(None, "field", None),
        P("field"),
        P("field", None),
        P("field", None, None),
        P("field", None, None),
        P("field", None, None),
    )
    out_specs = (P("probe", None, "field", None), P("probe", None), P("field", None, None))
    return jax.shard_map(
        on_device, mesh=mesh, in_specs=in_specs, out_specs=out_specs, check_vma=False
    )
```

profile of v0, /device:TPU:0, one launch (start us, length us, event | category | flops | bytes accessed | tf_op | source)
XLA Modules:
  0.0 235.5 jit_solution(16700310639509512461)
XLA Ops:
  10.0 5.0 %collective-permute-start.1 = (f32[8,4,1,256]{3,2,1,0:T(1,128)S(1)}, f32[8,4,1,256]{3,2,1,0:T(1,128)S(1)}, u32[]{:S(2)}, u32[]{:S(2)}) collective-permute-start(f32[8,4,1,256]{3,2,1,0:T(1,128)S(1)} %get-tuple-element.44), channel_id=1, source_target_pairs={{2,0},{4,2},{6,4},{8,6},{10,8},{12,10},{14,12},{16,14},{18,16},{20... | collective-permute-start | bytes 98312 | tf_op jit(solution)/shard_map/ppermute | solution.py:21
  20.4 4.4 %collective-permute-start.3 = (f32[8,4,1,256]{3,2,1,0:T(1,128)S(1)}, f32[8,4,1,256]{3,2,1,0:T(1,128)S(1)}, u32[]{:S(2)}, u32[]{:S(2)}) collective-permute-start(f32[8,4,1,256]{3,2,1,0:T(1,128)S(1)} %get-tuple-element.42), channel_id=1, source_target_pairs={{2,0},{4,2},{6,4},{8,6},{10,8},{12,10},{14,12},{16,14},{18,16},{20... | collective-permute-start | bytes 98312 | tf_op jit(solution)/shard_map/ppermute | solution.py:21
  27.2 4.5 %collective-permute-start.5 = (f32[8,4,1,256]{3,2,1,0:T(1,128)S(1)}, f32[8,4,1,256]{3,2,1,0:T(1,128)S(1)}, u32[]{:S(2)}, u32[]{:S(2)}) collective-permute-start(f32[8,4,1,256]{3,2,1,0:T(1,128)S(1)} %get-tuple-element.40), channel_id=1, source_target_pairs={{2,0},{4,2},{6,4},{8,6},{10,8},{12,10},{14,12},{16,14},{18,16},{20... | collective-permute-start | bytes 98312 | tf_op jit(solution)/shard_map/ppermute | solution.py:21
  34.2 4.4 %collective-permute-start.7 = (f32[8,4,1,256]{3,2,1,0:T(1,128)S(1)}, f32[8,4,1,256]{3,2,1,0:T(1,128)S(1)}, u32[]{:S(2)}, u32[]{:S(2)}) collective-permute-start(f32[8,4,1,256]{3,2,1,0:T(1,128)S(1)} %get-tuple-element.38), channel_id=1, source_target_pairs={{2,0},{4,2},{6,4},{8,6},{10,8},{12,10},{14,12},{16,14},{18,16},{20... | collective-permute-start | bytes 98312 | tf_op jit(solution)/shard_map/ppermute | solution.py:21
  41.2 4.5 %collective-permute-start.9 = (f32[8,4,2,256]{3,2,1,0:T(2,128)S(1)}, f32[8,4,2,256]{3,2,1,0:T(2,128)S(1)}, u32[]{:S(2)}, u32[]{:S(2)}) collective-permute-start(f32[8,4,2,256]{3,2,1,0:T(2,128)S(1)} %get-tuple-element.36), channel_id=1, source_target_pairs={{2,0},{4,2},{6,4},{8,6},{10,8},{12,10},{14,12},{16,14},{18,16},{20... | collective-permute-start | bytes 196616 | tf_op jit(solution)/shard_map/ppermute | solution.py:21
  49.8 4.5 %collective-permute-start.13 = (f32[8,4,2,256]{3,2,1,0:T(2,128)S(1)}, f32[8,4,2,256]{3,2,1,0:T(2,128)S(1)}, u32[]{:S(2)}, u32[]{:S(2)}) collective-permute-start(f32[8,4,2,256]{3,2,1,0:T(2,128)S(1)} %get-tuple-element.34), channel_id=1, source_target_pairs={{2,0},{4,2},{6,4},{8,6},{10,8},{12,10},{14,12},{16,14},{18,16},{20... | collective-permute-start | bytes 196616 | tf_op jit(solution)/shard_map/ppermute | solution.py:21
  58.4 4.7 %collective-permute-start.15 = (f32[8,4,2,256]{3,2,1,0:T(2,128)S(1)}, f32[8,4,2,256]{3,2,1,0:T(2,128)S(1)}, u32[]{:S(2)}, u32[]{:S(2)}) collective-permute-start(f32[8,4,2,256]{3,2,1,0:T(2,128)S(1)} %get-tuple-element.32), channel_id=1, source_target_pairs={{2,0},{4,2},{6,4},{8,6},{10,8},{12,10},{14,12},{16,14},{18,16},{20... | collective-permute-start | bytes 196616 | tf_op jit(solution)/shard_map/ppermute | solution.py:21
  67.1 8.6 %copy.46 = f32[8,4,32,256]{0,3,2,1:T(8,128)} copy(f32[8,4,32,256]{3,2,1,0:T(8,128)S(1)} %fusion.88) | data formatting | bytes 2097152 | tf_op jit(solution)/shard_map/sub | solution.py:77
  75.7 6.5 %gather_fusion = f32[256,8]{1,0:T(8,128)S(1)} fusion(f32[8,32768]{0,1:T(8,128)} %bitcast.35, s32[1024]{0:T(1024)S(1)} %pad_clamp_fusion), kind=kCustom, calls=%fused_computation | custom fusion | bytes 17408 | tf_op jit(solution)/shard_map/jit(_take)/gather | solution.py:94
  83.4 5.9 %all-to-all-start = ((f32[16,1,192]{2,1,0:T(1,128)}), f32[16,1,192]{2,1,0:T(1,128)S(1)}, u32[]{:S(2)}, u32[]{:S(2)}) async-start(f32[16,1,192]{2,1,0:T(1,128)} %reshape.115), calls=%async_computation | async-start | bytes 32768 | tf_op jit(solution)/shard_map/all_to_all | solution.py:99
  89.4 6.4 %all-to-all-done = f32[16,1,192]{2,1,0:T(1,128)S(1)} async-done(((f32[16,1,192]{2,1,0:T(1,128)}), f32[16,1,192]{2,1,0:T(1,128)S(1)}, u32[]{:S(2)}, u32[]{:S(2)}) %all-to-all-start) | async-done | bytes 12320 | tf_op jit(solution)/shard_map/all_to_all | solution.py:99
  97.2 9.1 %all_to_all.10 = f32[16,1,192]{2,1,0:T(1,128)S(1)} all-to-all(f32[16,1,192]{2,1,0:T(1,128)S(1)} %reshape.117), channel_id=1, replica_groups=mesh['field'=16,'probe'=2] {'field'}, dimensions={0} | all-to-all | bytes 24576 | tf_op jit(solution)/shard_map/all_to_all | solution.py:103
  107.6 8.2 %scatter_custom_fusion = f32[8,32768]{0,1:T(8,128)} fusion(s32[256]{0:T(256)S(1)} %bitcast.43, f32[256,8]{1,0:T(8,128)S(1)} %fusion.154, f32[]{:T(128)} %constant.10.clone.1), kind=kCustom, calls=%fused_computation.2 | custom fusion | flops 2048 | bytes 1048580 | tf_op jit(solution)/shard_map/scatter-add | solution.py:110
  115.8 9.8 %copy.50 = f32[8,4,32,256]{3,2,1,0:T(8,128)S(1)} copy(f32[8,4,32,256]{0,3,2,1:T(8,128)} %bitcast.34) | data formatting | bytes 2097152 | tf_op jit(solution)/shard_map/reshape | solution.py:111
  125.8 4.4 %collective-permute-start.17 = (f32[8,4,2,256]{3,2,1,0:T(2,128)S(1)}, f32[8,4,2,256]{3,2,1,0:T(2,128)S(1)}, u32[]{:S(2)}, u32[]{:S(2)}) collective-permute-start(f32[8,4,2,256]{3,2,1,0:T(2,128)S(1)} %get-tuple-element.30), channel_id=1, source_target_pairs={{2,0},{4,2},{6,4},{8,6},{10,8},{12,10},{14,12},{16,14},{18,16},{20... | collective-permute-start | bytes 196616 | tf_op jit(solution)/shard_map/ppermute | solution.py:21
  134.9 4.7 %collective-permute-start.19 = (f32[8,4,2,256]{3,2,1,0:T(2,128)S(1)}, f32[8,4,2,256]{3,2,1,0:T(2,128)S(1)}, u32[]{:S(2)}, u32[]{:S(2)}) collective-permute-start(f32[8,4,2,256]{3,2,1,0:T(2,128)S(1)} %get-tuple-element.28), channel_id=1, source_target_pairs={{2,0},{4,2},{6,4},{8,6},{10,8},{12,10},{14,12},{16,14},{18,16},{20... | collective-permute-start | bytes 196616 | tf_op jit(solution)/shard_map/ppermute | solution.py:21
  144.2 4.5 %collective-permute-start.21 = (f32[8,4,2,256]{3,2,1,0:T(2,128)S(1)}, f32[8,4,2,256]{3,2,1,0:T(2,128)S(1)}, u32[]{:S(2)}, u32[]{:S(2)}) collective-permute-start(f32[8,4,2,256]{3,2,1,0:T(2,128)S(1)} %get-tuple-element.26), channel_id=1, source_target_pairs={{2,0},{4,2},{6,4},{8,6},{10,8},{12,10},{14,12},{16,14},{18,16},{20... | collective-permute-start | bytes 196616 | tf_op jit(solution)/shard_map/ppermute | solution.py:21
  153.4 4.5 %collective-permute-start.23 = (f32[8,4,1,256]{3,2,1,0:T(1,128)S(1)}, f32[8,4,1,256]{3,2,1,0:T(1,128)S(1)}, u32[]{:S(2)}, u32[]{:S(2)}) collective-permute-start(f32[8,4,1,256]{3,2,1,0:T(1,128)S(1)} %get-tuple-element.24), channel_id=1, source_target_pairs={{2,0},{4,2},{6,4},{8,6},{10,8},{12,10},{14,12},{16,14},{18,16},{20... | collective-permute-start | bytes 98312 | tf_op jit(solution)/shard_map/ppermute | solution.py:21
  160.4 4.6 %collective-permute-start.25 = (f32[8,4,1,256]{3,2,1,0:T(1,128)S(1)}, f32[8,4,1,256]{3,2,1,0:T(1,128)S(1)}, u32[]{:S(2)}, u32[]{:S(2)}) collective-permute-start(f32[8,4,1,256]{3,2,1,0:T(1,128)S(1)} %get-tuple-element.22), channel_id=1, source_target_pairs={{2,0},{4,2},{6,4},{8,6},{10,8},{12,10},{14,12},{16,14},{18,16},{20... | collective-permute-start | bytes 98312 | tf_op jit(solution)/shard_map/ppermute | solution.py:21
  167.4 4.5 %collective-permute-start.27 = (f32[8,4,1,256]{3,2,1,0:T(1,128)S(1)}, f32[8,4,1,256]{3,2,1,0:T(1,128)S(1)}, u32[]{:S(2)}, u32[]{:S(2)}) collective-permute-start(f32[8,4,1,256]{3,2,1,0:T(1,128)S(1)} %get-tuple-element.20), channel_id=1, source_target_pairs={{2,0},{4,2},{6,4},{8,6},{10,8},{12,10},{14,12},{16,14},{18,16},{20... | collective-permute-start | bytes 98312 | tf_op jit(solution)/shard_map/ppermute | solution.py:21
  173.0 5.0 %psum.15 = f32[16,24]{1,0:T(8,128)S(1)} all-reduce(f32[16,24]{1,0:T(8,128)S(1)} %get-tuple-element.47), channel_id=1, replica_groups=mesh['field'=16,'probe'=2] {'probe'}, use_global_device_ids=true, to_apply=%region_4.5 | all-reduce | flops 384 | bytes 3072 | tf_op jit(solution)/shard_map/psum | solution.py:134
  178.8 4.4 %collective-permute-start.29 = (f32[8,4,1,256]{3,2,1,0:T(1,128)S(1)}, f32[8,4,1,256]{3,2,1,0:T(1,128)S(1)}, u32[]{:S(2)}, u32[]{:S(2)}) collective-permute-start(f32[8,4,1,256]{3,2,1,0:T(1,128)S(1)} %get-tuple-element.18), channel_id=1, source_target_pairs={{2,0},{4,2},{6,4},{8,6},{10,8},{12,10},{14,12},{16,14},{18,16},{20... | collective-permute-start | bytes 98312 | tf_op jit(solution)/shard_map/ppermute | solution.py:21
  185.6 6.6 %all-gather.2.cloned.1.call-done = bf16[16,4,32,256]{3,0,2,1:T(8,128)(2,1)} async-done(((bf16[8,4,32,256]{3,0,2,1:T(8,128)(2,1)}), bf16[16,4,32,256]{3,0,2,1:T(8,128)(2,1)}) %all-gather.2.cloned.1.call-update) | async-done | bytes 1048592 | tf_op jit(solution)/shard_map/all_gather | solution.py:126
  195.0 33.0 %psum.14 = f32[8,16]{1,0:T(8,128)S(1)} all-reduce(f32[8,16]{1,0:T(8,128)S(1)} %convolution_bitcast_fusion), channel_id=1, replica_groups=mesh['field'=16,'probe'=2] {'field'}, use_global_device_ids=true, to_apply=%region_2.3 | all-reduce | flops 128 | bytes 1024 | tf_op jit(solution)/shard_map/psum | solution.py:132
  (140 shorter events, 57.3 us)
Async XLA Ops:
  9.4 10.1 %collective-permute-start = (f32[8,4,1,256]{3,2,1,0:T(1,128)S(1)}, f32[8,4,1,256]{3,2,1,0:T(1,128)S(1)}, u32[]{:S(2)}, u32[]{:S(2)}) collective-permute-start(f32[8,4,1,256]{3,2,1,0:T(1,128)S(1)} %get-tuple-element.43), channel_id=1, source_target_pairs={{0,2},{2,4},{4,6},{6,8},{8,10},{10,12},{12,14},{14,16},{16,18},{18... | collective-permute-start | bytes 98312 | tf_op jit(solution)/shard_map/ppermute | solution.py:20
  10.0 9.6 %collective-permute-start.1 = (f32[8,4,1,256]{3,2,1,0:T(1,128)S(1)}, f32[8,4,1,256]{3,2,1,0:T(1,128)S(1)}, u32[]{:S(2)}, u32[]{:S(2)}) collective-permute-start(f32[8,4,1,256]{3,2,1,0:T(1,128)S(1)} %get-tuple-element.44), channel_id=1, source_target_pairs={{2,0},{4,2},{6,4},{8,6},{10,8},{12,10},{14,12},{16,14},{18,16},{20... | collective-permute-start | bytes 98312 | tf_op jit(solution)/shard_map/ppermute | solution.py:21
  15.0 30.7 %collective-permute-start.10 = (f32[4,2,256]{2,1,0:T(2,128)S(1)}, f32[4,2,256]{2,1,0:T(2,128)S(1)}, u32[]{:S(2)}, u32[]{:S(2)}) collective-permute-start(f32[4,2,256]{2,1,0:T(2,128)S(1)} %get-tuple-element.45), channel_id=1, source_target_pairs={{0,2},{2,4},{4,6},{6,8},{8,10},{10,12},{12,14},{14,16},{16,18},{18... | collective-permute-start | bytes 24584 | tf_op jit(solution)/shard_map/ppermute | solution.py:20
  15.1 30.6 %collective-permute-start.11 = (f32[4,2,256]{2,1,0:T(2,128)S(1)}, f32[4,2,256]{2,1,0:T(2,128)S(1)}, u32[]{:S(2)}, u32[]{:S(2)}) collective-permute-start(f32[4,2,256]{2,1,0:T(2,128)S(1)} %get-tuple-element.46), channel_id=1, source_target_pairs={{2,0},{4,2},{6,4},{8,6},{10,8},{12,10},{14,12},{16,14},{18,16},{20... | collective-permute-start | bytes 24584 | tf_op jit(solution)/shard_map/ppermute | solution.py:21
  27.2 6.2 %collective-permute-start.4 = (f32[8,4,1,256]{3,2,1,0:T(1,128)S(1)}, f32[8,4,1,256]{3,2,1,0:T(1,128)S(1)}, u32[]{:S(2)}, u32[]{:S(2)}) collective-permute-start(f32[8,4,1,256]{3,2,1,0:T(1,128)S(1)} %get-tuple-element.39), channel_id=1, source_target_pairs={{0,2},{2,4},{4,6},{6,8},{8,10},{10,12},{12,14},{14,16},{16,18},{18... | collective-permute-start | bytes 98312 | tf_op jit(solution)/shard_map/ppermute | solution.py:20
  34.2 6.2 %collective-permute-start.6 = (f32[8,4,1,256]{3,2,1,0:T(1,128)S(1)}, f32[8,4,1,256]{3,2,1,0:T(1,128)S(1)}, u32[]{:S(2)}, u32[]{:S(2)}) collective-permute-start(f32[8,4,1,256]{3,2,1,0:T(1,128)S(1)} %get-tuple-element.37), channel_id=1, source_target_pairs={{0,2},{2,4},{4,6},{6,8},{8,10},{10,12},{12,14},{14,16},{16,18},{18... | collective-permute-start | bytes 98312 | tf_op jit(solution)/shard_map/ppermute | solution.py:20
  41.1 6.5 %collective-permute-start.8 = (f32[8,4,2,256]{3,2,1,0:T(2,128)S(1)}, f32[8,4,2,256]{3,2,1,0:T(2,128)S(1)}, u32[]{:S(2)}, u32[]{:S(2)}) collective-permute-start(f32[8,4,2,256]{3,2,1,0:T(2,128)S(1)} %get-tuple-element.35), channel_id=1, source_target_pairs={{0,2},{2,4},{4,6},{6,8},{8,10},{10,12},{12,14},{14,16},{16,18},{18... | collective-permute-start | bytes 196616 | tf_op jit(solution)/shard_map/ppermute | solution.py:20
  41.2 6.4 %collective-permute-start.9 = (f32[8,4,2,256]{3,2,1,0:T(2,128)S(1)}, f32[8,4,2,256]{3,2,1,0:T(2,128)S(1)}, u32[]{:S(2)}, u32[]{:S(2)}) collective-permute-start(f32[8,4,2,256]{3,2,1,0:T(2,128)S(1)} %get-tuple-element.36), channel_id=1, source_target_pairs={{2,0},{4,2},{6,4},{8,6},{10,8},{12,10},{14,12},{16,14},{18,16},{20... | collective-permute-start | bytes 196616 | tf_op jit(solution)/shard_map/ppermute | solution.py:21
  49.7 6.5 %collective-permute-start.12 = (f32[8,4,2,256]{3,2,1,0:T(2,128)S(1)}, f32[8,4,2,256]{3,2,1,0:T(2,128)S(1)}, u32[]{:S(2)}, u32[]{:S(2)}) collective-permute-start(f32[8,4,2,256]{3,2,1,0:T(2,128)S(1)} %get-tuple-element.33), channel_id=1, source_target_pairs={{0,2},{2,4},{4,6},{6,8},{8,10},{10,12},{12,14},{14,16},{16,18},{18... | collective-permute-start | bytes 196616 | tf_op jit(solution)/shard_map/ppermute | solution.py:20
  49.8 6.4 %collective-permute-start.13 = (f32[8,4,2,256]{3,2,1,0:T(2,128)S(1)}, f32[8,4,2,256]{3,2,1,0:T(2,128)S(1)}, u32[]{:S(2)}, u32[]{:S(2)}) collective-permute-start(f32[8,4,2,256]{3,2,1,0:T(2,128)S(1)} %get-tuple-element.34), channel_id=1, source_target_pairs={{2,0},{4,2},{6,4},{8,6},{10,8},{12,10},{14,12},{16,14},{18,16},{20... | collective-permute-start | bytes 196616 | tf_op jit(solution)/shard_map/ppermute | solution.py:21
  58.4 6.5 %collective-permute-start.14 = (f32[8,4,2,256]{3,2,1,0:T(2,128)S(1)}, f32[8,4,2,256]{3,2,1,0:T(2,128)S(1)}, u32[]{:S(2)}, u32[]{:S(2)}) collective-permute-start(f32[8,4,2,256]{3,2,1,0:T(2,128)S(1)} %get-tuple-element.31), channel_id=1, source_target_pairs={{0,2},{2,4},{4,6},{6,8},{8,10},{10,12},{12,14},{14,16},{16,18},{18... | collective-permute-start | bytes 196616 | tf_op jit(solution)/shard_map/ppermute | solution.py:20
  58.4 6.6 %collective-permute-start.15 = (f32[8,4,2,256]{3,2,1,0:T(2,128)S(1)}, f32[8,4,2,256]{3,2,1,0:T(2,128)S(1)}, u32[]{:S(2)}, u32[]{:S(2)}) collective-permute-start(f32[8,4,2,256]{3,2,1,0:T(2,128)S(1)} %get-tuple-element.32), channel_id=1, source_target_pairs={{2,0},{4,2},{6,4},{8,6},{10,8},{12,10},{14,12},{16,14},{18,16},{20... | collective-permute-start | bytes 196616 | tf_op jit(solution)/shard_map/ppermute | solution.py:21
  83.4 12.4 %all-to-all-start = ((f32[16,1,192]{2,1,0:T(1,128)}), f32[16,1,192]{2,1,0:T(1,128)S(1)}, u32[]{:S(2)}, u32[]{:S(2)}) async-start(f32[16,1,192]{2,1,0:T(1,128)} %reshape.115), calls=%async_computation | async-start | bytes 32768 | tf_op jit(solution)/shard_map/all_to_all | solution.py:99
  89.3 102.8 %all-gather.2.cloned.1.call-start = ((), (), s32[]{:S(2)}) async-start(), calls=%async_computation.2 | async-start | bytes 1572864 | tf_op jit(solution)/shard_map/all_gather | solution.py:126
  125.7 6.4 %collective-permute-start.16 = (f32[8,4,2,256]{3,2,1,0:T(2,128)S(1)}, f32[8,4,2,256]{3,2,1,0:T(2,128)S(1)}, u32[]{:S(2)}, u32[]{:S(2)}) collective-permute-start(f32[8,4,2,256]{3,2,1,0:T(2,128)S(1)} %get-tuple-element.29), channel_id=1, source_target_pairs={{0,2},{2,4},{4,6},{6,8},{8,10},{10,12},{12,14},{14,16},{16,18},{18... | collective-permute-start | bytes 196616 | tf_op jit(solution)/shard_map/ppermute | solution.py:20
  125.8 6.4 %collective-permute-start.17 = (f32[8,4,2,256]{3,2,1,0:T(2,128)S(1)}, f32[8,4,2,256]{3,2,1,0:T(2,128)S(1)}, u32[]{:S(2)}, u32[]{:S(2)}) collective-permute-start(f32[8,4,2,256]{3,2,1,0:T(2,128)S(1)} %get-tuple-element.30), channel_id=1, source_target_pairs={{2,0},{4,2},{6,4},{8,6},{10,8},{12,10},{14,12},{16,14},{18,16},{20... | collective-permute-start | bytes 196616 | tf_op jit(solution)/shard_map/ppermute | solution.py:21
  134.8 6.4 %collective-permute-start.18 = (f32[8,4,2,256]{3,2,1,0:T(2,128)S(1)}, f32[8,4,2,256]{3,2,1,0:T(2,128)S(1)}, u32[]{:S(2)}, u32[]{:S(2)}) collective-permute-start(f32[8,4,2,256]{3,2,1,0:T(2,128)S(1)} %get-tuple-element.27), channel_id=1, source_target_pairs={{0,2},{2,4},{4,6},{6,8},{8,10},{10,12},{12,14},{14,16},{16,18},{18... | collective-permute-start | bytes 196616 | tf_op jit(solution)/shard_map/ppermute | solution.py:20
  134.9 6.6 %collective-permute-start.19 = (f32[8,4,2,256]{3,2,1,0:T(2,128)S(1)}, f32[8,4,2,256]{3,2,1,0:T(2,128)S(1)}, u32[]{:S(2)}, u32[]{:S(2)}) collective-permute-start(f32[8,4,2,256]{3,2,1,0:T(2,128)S(1)} %get-tuple-element.28), channel_id=1, source_target_pairs={{2,0},{4,2},{6,4},{8,6},{10,8},{12,10},{14,12},{16,14},{18,16},{20... | collective-permute-start | bytes 196616 | tf_op jit(solution)/shard_map/ppermute | solution.py:21
  144.1 6.5 %collective-permute-start.20 = (f32[8,4,2,256]{3,2,1,0:T(2,128)S(1)}, f32[8,4,2,256]{3,2,1,0:T(2,128)S(1)}, u32[]{:S(2)}, u32[]{:S(2)}) collective-permute-start(f32[8,4,2,256]{3,2,1,0:T(2,128)S(1)} %get-tuple-element.25), channel_id=1, source_target_pairs={{0,2},{2,4},{4,6},{6,8},{8,10},{10,12},{12,14},{14,16},{16,18},{18... | collective-permute-start | bytes 196616 | tf_op jit(solution)/shard_map/ppermute | solution.py:20
  144.2 6.4 %collective-permute-start.21 = (f32[8,4,2,256]{3,2,1,0:T(2,128)S(1)}, f32[8,4,2,256]{3,2,1,0:T(2,128)S(1)}, u32[]{:S(2)}, u32[]{:S(2)}) collective-permute-start(f32[8,4,2,256]{3,2,1,0:T(2,128)S(1)} %get-tuple-element.26), channel_id=1, source_target_pairs={{2,0},{4,2},{6,4},{8,6},{10,8},{12,10},{14,12},{16,14},{18,16},{20... | collective-permute-start | bytes 196616 | tf_op jit(solution)/shard_map/ppermute | solution.py:21
  153.3 6.2 %collective-permute-start.22 = (f32[8,4,1,256]{3,2,1,0:T(1,128)S(1)}, f32[8,4,1,256]{3,2,1,0:T(1,128)S(1)}, u32[]{:S(2)}, u32[]{:S(2)}) collective-permute-start(f32[8,4,1,256]{3,2,1,0:T(1,128)S(1)} %get-tuple-element.23), channel_id=1, source_target_pairs={{0,2},{2,4},{4,6},{6,8},{8,10},{10,12},{12,14},{14,16},{16,18},{18... | collective-permute-start | bytes 98312 | tf_op jit(solution)/shard_map/ppermute | solution.py:20
  160.3 6.2 %collective-permute-start.24 = (f32[8,4,1,256]{3,2,1,0:T(1,128)S(1)}, f32[8,4,1,256]{3,2,1,0:T(1,128)S(1)}, u32[]{:S(2)}, u32[]{:S(2)}) collective-permute-start(f32[8,4,1,256]{3,2,1,0:T(1,128)S(1)} %get-tuple-element.21), channel_id=1, source_target_pairs={{0,2},{2,4},{4,6},{6,8},{8,10},{10,12},{12,14},{14,16},{16,18},{18... | collective-permute-start | bytes 98312 | tf_op jit(solution)/shard_map/ppermute | solution.py:20
  167.4 10.7 %collective-permute-start.26 = (f32[8,4,1,256]{3,2,1,0:T(1,128)S(1)}, f32[8,4,1,256]{3,2,1,0:T(1,128)S(1)}, u32[]{:S(2)}, u32[]{:S(2)}) collective-permute-start(f32[8,4,1,256]{3,2,1,0:T(1,128)S(1)} %get-tuple-element.19), channel_id=1, source_target_pairs={{0,2},{2,4},{4,6},{6,8},{8,10},{10,12},{12,14},{14,16},{16,18},{18... | collective-permute-start | bytes 98312 | tf_op jit(solution)/shard_map/ppermute | solution.py:20
  167.4 10.6 %collective-permute-start.27 = (f32[8,4,1,256]{3,2,1,0:T(1,128)S(1)}, f32[8,4,1,256]{3,2,1,0:T(1,128)S(1)}, u32[]{:S(2)}, u32[]{:S(2)}) collective-permute-start(f32[8,4,1,256]{3,2,1,0:T(1,128)S(1)} %get-tuple-element.20), channel_id=1, source_target_pairs={{2,0},{4,2},{6,4},{8,6},{10,8},{12,10},{14,12},{16,14},{18,16},{20... | collective-permute-start | bytes 98312 | tf_op jit(solution)/shard_map/ppermute | solution.py:21
  (15 other events, 172.6 us)
Sparse Core Ops, SparseCore 0:
  173.1 18.9 all-gather.1
where the time goes:
time: 236 us
  starting transfers between devices  75.5 us (32%)
  blocking collectives  47.1 us (20%)
  waiting for transfers between devices  32.7 us (14%)
  other arithmetic  31.7 us (13%)
  local copies, waits for them, and re-layouts  29.5 us (12%)
  between operations  15.3 us (6%)
  matrix products  3.61 us (2%)
    ppermute x15, starting transfers between devices, with_halo(): after = lax.ppermute(first, axis, down)  68.3 us
    psum x1, blocking collectives, on_device(): tiles = lax.psum(columns, 'field') * scale_factor  33 us
    ppermute x15, waiting for transfers between devices, with_halo(): before = lax.ppermute(last, axis, up)  19.2 us
    reshape x1, local copies, waits for them, and re-layouts, on_device(): adjoint = injected.reshape(probes.shape)  9.83 us
    all_to_all x1, blocking collectives, on_device(): lax.all_to_all(weighted, 'field', split_axis=0, concat_axis=0, tiled=True)  9.07 us
    sub x1, local copies, waits for them, and re-layouts, on_device(): middle + coef_mid * (beside_all - 6.0 * middle)  8.58 us
    scatter-add x1, other arithmetic, on_device(): jnp.zeros((probe_count, cell_count), jnp.float32).at[:, cells]  8.2 us
    all_gather x1, waiting for transfers between devices, on_device(): piece = lax.all_gather(probes, 'probe', axis=0, tiled=True)  6.56 us
  transfers between devices with their start and end apart: 32, of which 16 were waited for; matrix products, arithmetic and copies ran while one was open for 3% of the time, Pallas kernels for 0%

commit v1 on v0

--- a/solution.py
+++ b/solution.py
@@ -1,13 +1,42 @@
+import functools
 import math
 import jax
 import jax.numpy as jnp
 from jax import lax
 from jax.sharding import PartitionSpec as P
+from jax.lax import axis_index, axis_size, ppermute
 
 SWEEPS = 4
 STEPS = 6
 SENS_DEV = 160
 advect_speed = 0.3
+
+
+def pack_the_tasks(obj, at_axis):
+    formed = list(obj.shape[1:])
+    formed[at_axis] *= obj.shape[0]
+    return jnp.moveaxis(obj, 0, at_axis).reshape(formed)
+
+
+def plane_touch(unit, mesh_name):
+    full_n = axis_size(mesh_name)
+    now = unit[None]
+    for to_i in range(full_n.bit_length() - 1):
+        local_next = 1 << to_i
+        part_now = ppermute(
+            now, axis_name=mesh_name, perm=tuple(((ix, ix ^ local_next) for ix in range(full_n)))
+        )
+        item_now = jnp.stack([now, part_now])
+        arr_next = axis_index(mesh_name) >> to_i & 1
+        now = jnp.where(arr_next == 0, item_now, item_now[::-1]).reshape(-1, *unit.shape)
+    return now
+
+
+def recover_ports_now(point, raw, out_dim):
+    return pack_the_tasks(plane_touch(point, raw), out_dim)
+
+
+_post_vectors = functools.partial(recover_ports_now, raw="probe", out_dim=0)
 
 
 def with_halo(value, sides, width):
@@ -123,7 +152,7 @@
         adjoint = extended
     hessian_probes = prior_apply(adjoint, diagonal)
     flat_result = hessian_probes.reshape(probe_count, cell_count)
-    piece = lax.all_gather(probes, "probe", axis=0, tiled=True)
+    piece = _post_vectors(probes)
     flat_piece = piece.reshape(piece.shape[0], cell_count).astype(jnp.float32)
     columns = lax.dot_general(
         flat_result, flat_piece, (((1,), (1,)), ((), ())), precision=lax.Precision.HIGHEST

time: 236 us -> 221 us (0.936)
  between operations: 15.3 us -> 1.97 us
  waiting for transfers between devices: 32.7 us -> 24.6 us
  local copies, waits for them, and re-layouts: 29.5 us -> 32.4 us
    all_gather x1 -> x0, waiting for transfers between devices: 6.56 us -> none  [on_device(): piece = lax.all_gather(probes, 'probe', axis=0, tiled=True)]
    psum x1, blocking collectives: 5 us -> 8.3 us  [on_device(): total_squares = lax.psum(squares, 'probe')]
  transfers between devices with their start and end apart: 32 -> 32, of which waited for: 16 -> 13; matrix products, arithmetic and copies ran while one was open for 3% -> 4% of each run, Pallas kernels for 0% -> 0%
where the time goes in v1:
time: 221 us
  starting transfers between devices  77.3 us (35%)
  blocking collectives  49.3 us (22%)
  other arithmetic  33.1 us (15%)
  local copies, waits for them, and re-layouts  32.4 us (15%)
  waiting for transfers between devices  24.6 us (11%)
    ppermute x15, starting transfers between devices, with_halo(): after = lax.ppermute(first, axis, down)  67.9 us
    psum x1, blocking collectives, on_device(): tiles = lax.psum(columns, 'field') * scale_factor  31.9 us
    ppermute x15, waiting for transfers between devices, with_halo(): before = lax.ppermute(last, axis, up)  17.8 us
    reshape x1, local copies, waits for them, and re-layouts, on_device(): adjoint = injected.reshape(probes.shape)  9.83 us
    all_to_all x1, blocking collectives, on_device(): lax.all_to_all(weighted, 'field', split_axis=0, concat_axis=0, tiled=True)  9.07 us
    sub x1, local copies, waits for them, and re-layouts, on_device(): middle + coef_mid * (beside_all - 6.0 * middle)  8.58 us
    psum x1, blocking collectives, on_device(): total_squares = lax.psum(squares, 'probe')  8.3 us
    scatter-add x1, other arithmetic, on_device(): jnp.zeros((probe_count, cell_count), jnp.float32).at[:, cells]  8.21 us
  transfers between devices with their start and end apart: 32, of which 13 were waited for; matrix products, arithmetic and copies ran while one was open for 4% of the time, Pallas kernels for 0%

profile of v1, /device:TPU:0, one launch (start us, length us, event | category | flops | bytes accessed | tf_op | source)
XLA Modules:
  0.0 220.6 jit_solution(10343671269348558344)
XLA Ops:
  3.4 5.0 %collective-permute-start.1 = (f32[8,4,1,256]{3,2,1,0:T(1,128)S(1)}, f32[8,4,1,256]{3,2,1,0:T(1,128)S(1)}, u32[]{:S(2)}, u32[]{:S(2)}) collective-permute-start(f32[8,4,1,256]{3,2,1,0:T(1,128)S(1)} %get-tuple-element.44), channel_id=1, source_target_pairs={{2,0},{4,2},{6,4},{8,6},{10,8},{12,10},{14,12},{16,14},{18,16},{20... | collective-permute-start | bytes 98312 | tf_op jit(solution)/shard_map/ppermute | solution.py:50
  8.6 4.4 %collective-permute-start.11 = (f32[4,2,256]{2,1,0:T(2,128)S(1)}, f32[4,2,256]{2,1,0:T(2,128)S(1)}, u32[]{:S(2)}, u32[]{:S(2)}) collective-permute-start(f32[4,2,256]{2,1,0:T(2,128)S(1)} %get-tuple-element.46), channel_id=1, source_target_pairs={{2,0},{4,2},{6,4},{8,6},{10,8},{12,10},{14,12},{16,14},{18,16},{20... | collective-permute-start | bytes 24584 | tf_op jit(solution)/shard_map/ppermute | solution.py:50
  13.8 4.4 %collective-permute-start.3 = (f32[8,4,1,256]{3,2,1,0:T(1,128)S(1)}, f32[8,4,1,256]{3,2,1,0:T(1,128)S(1)}, u32[]{:S(2)}, u32[]{:S(2)}) collective-permute-start(f32[8,4,1,256]{3,2,1,0:T(1,128)S(1)} %get-tuple-element.42), channel_id=1, source_target_pairs={{2,0},{4,2},{6,4},{8,6},{10,8},{12,10},{14,12},{16,14},{18,16},{20... | collective-permute-start | bytes 98312 | tf_op jit(solution)/shard_map/ppermute | solution.py:50
  20.7 4.5 %collective-permute-start.5 = (f32[8,4,1,256]{3,2,1,0:T(1,128)S(1)}, f32[8,4,1,256]{3,2,1,0:T(1,128)S(1)}, u32[]{:S(2)}, u32[]{:S(2)}) collective-permute-start(f32[8,4,1,256]{3,2,1,0:T(1,128)S(1)} %get-tuple-element.40), channel_id=1, source_target_pairs={{2,0},{4,2},{6,4},{8,6},{10,8},{12,10},{14,12},{16,14},{18,16},{20... | collective-permute-start | bytes 98312 | tf_op jit(solution)/shard_map/ppermute | solution.py:50
  27.7 4.4 %collective-permute-start.7 = (f32[8,4,1,256]{3,2,1,0:T(1,128)S(1)}, f32[8,4,1,256]{3,2,1,0:T(1,128)S(1)}, u32[]{:S(2)}, u32[]{:S(2)}) collective-permute-start(f32[8,4,1,256]{3,2,1,0:T(1,128)S(1)} %get-tuple-element.38), channel_id=1, source_target_pairs={{2,0},{4,2},{6,4},{8,6},{10,8},{12,10},{14,12},{16,14},{18,16},{20... | collective-permute-start | bytes 98312 | tf_op jit(solution)/shard_map/ppermute | solution.py:50
  34.7 4.5 %collective-permute-start.9 = (f32[8,4,2,256]{3,2,1,0:T(2,128)S(1)}, f32[8,4,2,256]{3,2,1,0:T(2,128)S(1)}, u32[]{:S(2)}, u32[]{:S(2)}) collective-permute-start(f32[8,4,2,256]{3,2,1,0:T(2,128)S(1)} %get-tuple-element.36), channel_id=1, source_target_pairs={{2,0},{4,2},{6,4},{8,6},{10,8},{12,10},{14,12},{16,14},{18,16},{20... | collective-permute-start | bytes 196616 | tf_op jit(solution)/shard_map/ppermute | solution.py:50
  43.3 4.5 %collective-permute-start.13 = (f32[8,4,2,256]{3,2,1,0:T(2,128)S(1)}, f32[8,4,2,256]{3,2,1,0:T(2,128)S(1)}, u32[]{:S(2)}, u32[]{:S(2)}) collective-permute-start(f32[8,4,2,256]{3,2,1,0:T(2,128)S(1)} %get-tuple-element.34), channel_id=1, source_target_pairs={{2,0},{4,2},{6,4},{8,6},{10,8},{12,10},{14,12},{16,14},{18,16},{20... | collective-permute-start | bytes 196616 | tf_op jit(solution)/shard_map/ppermute | solution.py:50
  52.0 4.5 %collective-permute-start.15 = (f32[8,4,2,256]{3,2,1,0:T(2,128)S(1)}, f32[8,4,2,256]{3,2,1,0:T(2,128)S(1)}, u32[]{:S(2)}, u32[]{:S(2)}) collective-permute-start(f32[8,4,2,256]{3,2,1,0:T(2,128)S(1)} %get-tuple-element.32), channel_id=1, source_target_pairs={{2,0},{4,2},{6,4},{8,6},{10,8},{12,10},{14,12},{16,14},{18,16},{20... | collective-permute-start | bytes 196616 | tf_op jit(solution)/shard_map/ppermute | solution.py:50
  60.5 8.6 %copy.38 = f32[8,4,32,256]{0,3,2,1:T(8,128)} copy(f32[8,4,32,256]{3,2,1,0:T(8,128)S(1)} %fusion.88) | data formatting | bytes 2097152 | tf_op jit(solution)/shard_map/sub | solution.py:106
  69.1 6.5 %gather_fusion = f32[256,8]{1,0:T(8,128)S(1)} fusion(f32[8,32768]{0,1:T(8,128)} %bitcast.42, s32[1024]{0:T(1024)S(1)} %pad_clamp_fusion), kind=kCustom, calls=%fused_computation | custom fusion | bytes 17408 | tf_op jit(solution)/shard_map/jit(_take)/gather | solution.py:123
  76.8 6.0 %all-to-all-start = ((f32[16,1,192]{2,1,0:T(1,128)}), f32[16,1,192]{2,1,0:T(1,128)S(1)}, u32[]{:S(2)}, u32[]{:S(2)}) async-start(f32[16,1,192]{2,1,0:T(1,128)} %reshape.116), calls=%async_computation | async-start | bytes 32768 | tf_op jit(solution)/shard_map/all_to_all | solution.py:128
  82.9 6.5 %all-to-all-done = f32[16,1,192]{2,1,0:T(1,128)S(1)} async-done(((f32[16,1,192]{2,1,0:T(1,128)}), f32[16,1,192]{2,1,0:T(1,128)S(1)}, u32[]{:S(2)}, u32[]{:S(2)}) %all-to-all-start) | async-done | bytes 12320 | tf_op jit(solution)/shard_map/all_to_all | solution.py:128
  90.8 9.1 %all_to_all.10 = f32[16,1,192]{2,1,0:T(1,128)S(1)} all-to-all(f32[16,1,192]{2,1,0:T(1,128)S(1)} %reshape.118), channel_id=1, replica_groups=mesh['field'=16,'probe'=2] {'field'}, dimensions={0} | all-to-all | bytes 24576 | tf_op jit(solution)/shard_map/all_to_all | solution.py:132
  101.2 8.2 %scatter_custom_fusion = f32[8,32768]{0,1:T(8,128)} fusion(s32[256]{0:T(256)S(1)} %bitcast.53, f32[256,8]{1,0:T(8,128)S(1)} %fusion.153, f32[]{:T(128)} %constant.12.clone.1), kind=kCustom, calls=%fused_computation.2 | custom fusion | flops 2048 | bytes 1048580 | tf_op jit(solution)/shard_map/scatter-add | solution.py:139
  109.4 9.8 %copy.42 = f32[8,4,32,256]{3,2,1,0:T(8,128)S(1)} copy(f32[8,4,32,256]{0,3,2,1:T(8,128)} %bitcast.39) | data formatting | bytes 2097152 | tf_op jit(solution)/shard_map/reshape | solution.py:140
  119.3 4.4 %collective-permute-start.17 = (f32[8,4,2,256]{3,2,1,0:T(2,128)S(1)}, f32[8,4,2,256]{3,2,1,0:T(2,128)S(1)}, u32[]{:S(2)}, u32[]{:S(2)}) collective-permute-start(f32[8,4,2,256]{3,2,1,0:T(2,128)S(1)} %get-tuple-element.30), channel_id=1, source_target_pairs={{2,0},{4,2},{6,4},{8,6},{10,8},{12,10},{14,12},{16,14},{18,16},{20... | collective-permute-start | bytes 196616 | tf_op jit(solution)/shard_map/ppermute | solution.py:50
  128.5 4.5 %collective-permute-start.19 = (f32[8,4,2,256]{3,2,1,0:T(2,128)S(1)}, f32[8,4,2,256]{3,2,1,0:T(2,128)S(1)}, u32[]{:S(2)}, u32[]{:S(2)}) collective-permute-start(f32[8,4,2,256]{3,2,1,0:T(2,128)S(1)} %get-tuple-element.28), channel_id=1, source_target_pairs={{2,0},{4,2},{6,4},{8,6},{10,8},{12,10},{14,12},{16,14},{18,16},{20... | collective-permute-start | bytes 196616 | tf_op jit(solution)/shard_map/ppermute | solution.py:50
  137.5 4.8 %collective-permute-start.21 = (f32[8,4,2,256]{3,2,1,0:T(2,128)S(1)}, f32[8,4,2,256]{3,2,1,0:T(2,128)S(1)}, u32[]{:S(2)}, u32[]{:S(2)}) collective-permute-start(f32[8,4,2,256]{3,2,1,0:T(2,128)S(1)} %get-tuple-element.26), channel_id=1, source_target_pairs={{2,0},{4,2},{6,4},{8,6},{10,8},{12,10},{14,12},{16,14},{18,16},{20... | collective-permute-start | bytes 196616 | tf_op jit(solution)/shard_map/ppermute | solution.py:50
  147.0 4.5 %collective-permute-start.23 = (f32[8,4,1,256]{3,2,1,0:T(1,128)S(1)}, f32[8,4,1,256]{3,2,1,0:T(1,128)S(1)}, u32[]{:S(2)}, u32[]{:S(2)}) collective-permute-start(f32[8,4,1,256]{3,2,1,0:T(1,128)S(1)} %get-tuple-element.24), channel_id=1, source_target_pairs={{2,0},{4,2},{6,4},{8,6},{10,8},{12,10},{14,12},{16,14},{18,16},{20... | collective-permute-start | bytes 98312 | tf_op jit(solution)/shard_map/ppermute | solution.py:50
  153.5 8.3 %psum.15 = f32[16,24]{1,0:T(8,128)S(1)} all-reduce(f32[16,24]{1,0:T(8,128)S(1)} %get-tuple-element.47), channel_id=1, replica_groups=mesh['field'=16,'probe'=2] {'probe'}, use_global_device_ids=true, to_apply=%region_4.5 | all-reduce | flops 384 | bytes 3072 | tf_op jit(solution)/shard_map/psum | solution.py:163
  162.6 4.4 %collective-permute-start.25 = (f32[8,4,1,256]{3,2,1,0:T(1,128)S(1)}, f32[8,4,1,256]{3,2,1,0:T(1,128)S(1)}, u32[]{:S(2)}, u32[]{:S(2)}) collective-permute-start(f32[8,4,1,256]{3,2,1,0:T(1,128)S(1)} %get-tuple-element.22), channel_id=1, source_target_pairs={{2,0},{4,2},{6,4},{8,6},{10,8},{12,10},{14,12},{16,14},{18,16},{20... | collective-permute-start | bytes 98312 | tf_op jit(solution)/shard_map/ppermute | solution.py:50
  169.6 4.4 %collective-permute-start.27 = (f32[8,4,1,256]{3,2,1,0:T(1,128)S(1)}, f32[8,4,1,256]{3,2,1,0:T(1,128)S(1)}, u32[]{:S(2)}, u32[]{:S(2)}) collective-permute-start(f32[8,4,1,256]{3,2,1,0:T(1,128)S(1)} %get-tuple-element.20), channel_id=1, source_target_pairs={{2,0},{4,2},{6,4},{8,6},{10,8},{12,10},{14,12},{16,14},{18,16},{20... | collective-permute-start | bytes 98312 | tf_op jit(solution)/shard_map/ppermute | solution.py:50
  176.5 4.4 %collective-permute-start.29 = (f32[8,4,1,256]{3,2,1,0:T(1,128)S(1)}, f32[8,4,1,256]{3,2,1,0:T(1,128)S(1)}, u32[]{:S(2)}, u32[]{:S(2)}) collective-permute-start(f32[8,4,1,256]{3,2,1,0:T(1,128)S(1)} %get-tuple-element.18), channel_id=1, source_target_pairs={{2,0},{4,2},{6,4},{8,6},{10,8},{12,10},{14,12},{16,14},{18,16},{20... | collective-permute-start | bytes 98312 | tf_op jit(solution)/shard_map/ppermute | solution.py:50
  188.1 31.9 %psum.14 = f32[8,16]{1,0:T(8,128)S(1)} all-reduce(f32[8,16]{1,0:T(8,128)S(1)} %fusion.185), channel_id=1, replica_groups=mesh['field'=16,'probe'=2] {'field'}, use_global_device_ids=true, to_apply=%region_2.3 | all-reduce | flops 128 | bytes 1024 | tf_op jit(solution)/shard_map/psum | solution.py:161
  (144 shorter events, 55.8 us)
Async XLA Ops:
  2.9 10.1 %collective-permute-start = (f32[8,4,1,256]{3,2,1,0:T(1,128)S(1)}, f32[8,4,1,256]{3,2,1,0:T(1,128)S(1)}, u32[]{:S(2)}, u32[]{:S(2)}) collective-permute-start(f32[8,4,1,256]{3,2,1,0:T(1,128)S(1)} %get-tuple-element.43), channel_id=1, source_target_pairs={{0,2},{2,4},{4,6},{6,8},{8,10},{10,12},{12,14},{14,16},{16,18},{18... | collective-permute-start | bytes 98312 | tf_op jit(solution)/shard_map/ppermute | solution.py:49
  3.4 9.6 %collective-permute-start.1 = (f32[8,4,1,256]{3,2,1,0:T(1,128)S(1)}, f32[8,4,1,256]{3,2,1,0:T(1,128)S(1)}, u32[]{:S(2)}, u32[]{:S(2)}) collective-permute-start(f32[8,4,1,256]{3,2,1,0:T(1,128)S(1)} %get-tuple-element.44), channel_id=1, source_target_pairs={{2,0},{4,2},{6,4},{8,6},{10,8},{12,10},{14,12},{16,14},{18,16},{20... | collective-permute-start | bytes 98312 | tf_op jit(solution)/shard_map/ppermute | solution.py:50
  8.5 30.7 %collective-permute-start.10 = (f32[4,2,256]{2,1,0:T(2,128)S(1)}, f32[4,2,256]{2,1,0:T(2,128)S(1)}, u32[]{:S(2)}, u32[]{:S(2)}) collective-permute-start(f32[4,2,256]{2,1,0:T(2,128)S(1)} %get-tuple-element.45), channel_id=1, source_target_pairs={{0,2},{2,4},{4,6},{6,8},{8,10},{10,12},{12,14},{14,16},{16,18},{18... | collective-permute-start | bytes 24584 | tf_op jit(solution)/shard_map/ppermute | solution.py:49
  8.6 30.6 %collective-permute-start.11 = (f32[4,2,256]{2,1,0:T(2,128)S(1)}, f32[4,2,256]{2,1,0:T(2,128)S(1)}, u32[]{:S(2)}, u32[]{:S(2)}) collective-permute-start(f32[4,2,256]{2,1,0:T(2,128)S(1)} %get-tuple-element.46), channel_id=1, source_target_pairs={{2,0},{4,2},{6,4},{8,6},{10,8},{12,10},{14,12},{16,14},{18,16},{20... | collective-permute-start | bytes 24584 | tf_op jit(solution)/shard_map/ppermute | solution.py:50
  20.6 6.2 %collective-permute-start.4 = (f32[8,4,1,256]{3,2,1,0:T(1,128)S(1)}, f32[8,4,1,256]{3,2,1,0:T(1,128)S(1)}, u32[]{:S(2)}, u32[]{:S(2)}) collective-permute-start(f32[8,4,1,256]{3,2,1,0:T(1,128)S(1)} %get-tuple-element.39), channel_id=1, source_target_pairs={{0,2},{2,4},{4,6},{6,8},{8,10},{10,12},{12,14},{14,16},{16,18},{18... | collective-permute-start | bytes 98312 | tf_op jit(solution)/shard_map/ppermute | solution.py:49
  34.6 6.5 %collective-permute-start.8 = (f32[8,4,2,256]{3,2,1,0:T(2,128)S(1)}, f32[8,4,2,256]{3,2,1,0:T(2,128)S(1)}, u32[]{:S(2)}, u32[]{:S(2)}) collective-permute-start(f32[8,4,2,256]{3,2,1,0:T(2,128)S(1)} %get-tuple-element.35), channel_id=1, source_target_pairs={{0,2},{2,4},{4,6},{6,8},{8,10},{10,12},{12,14},{14,16},{16,18},{18... | collective-permute-start | bytes 196616 | tf_op jit(solution)/shard_map/ppermute | solution.py:49
  34.7 6.4 %collective-permute-start.9 = (f32[8,4,2,256]{3,2,1,0:T(2,128)S(1)}, f32[8,4,2,256]{3,2,1,0:T(2,128)S(1)}, u32[]{:S(2)}, u32[]{:S(2)}) collective-permute-start(f32[8,4,2,256]{3,2,1,0:T(2,128)S(1)} %get-tuple-element.36), channel_id=1, source_target_pairs={{2,0},{4,2},{6,4},{8,6},{10,8},{12,10},{14,12},{16,14},{18,16},{20... | collective-permute-start | bytes 196616 | tf_op jit(solution)/shard_map/ppermute | solution.py:50
  43.2 6.5 %collective-permute-start.12 = (f32[8,4,2,256]{3,2,1,0:T(2,128)S(1)}, f32[8,4,2,256]{3,2,1,0:T(2,128)S(1)}, u32[]{:S(2)}, u32[]{:S(2)}) collective-permute-start(f32[8,4,2,256]{3,2,1,0:T(2,128)S(1)} %get-tuple-element.33), channel_id=1, source_target_pairs={{0,2},{2,4},{4,6},{6,8},{8,10},{10,12},{12,14},{14,16},{16,18},{18... | collective-permute-start | bytes 196616 | tf_op jit(solution)/shard_map/ppermute | solution.py:49
  43.3 6.4 %collective-permute-start.13 = (f32[8,4,2,256]{3,2,1,0:T(2,128)S(1)}, f32[8,4,2,256]{3,2,1,0:T(2,128)S(1)}, u32[]{:S(2)}, u32[]{:S(2)}) collective-permute-start(f32[8,4,2,256]{3,2,1,0:T(2,128)S(1)} %get-tuple-element.34), channel_id=1, source_target_pairs={{2,0},{4,2},{6,4},{8,6},{10,8},{12,10},{14,12},{16,14},{18,16},{20... | collective-permute-start | bytes 196616 | tf_op jit(solution)/shard_map/ppermute | solution.py:50
  51.9 6.5 %collective-permute-start.14 = (f32[8,4,2,256]{3,2,1,0:T(2,128)S(1)}, f32[8,4,2,256]{3,2,1,0:T(2,128)S(1)}, u32[]{:S(2)}, u32[]{:S(2)}) collective-permute-start(f32[8,4,2,256]{3,2,1,0:T(2,128)S(1)} %get-tuple-element.31), channel_id=1, source_target_pairs={{0,2},{2,4},{4,6},{6,8},{8,10},{10,12},{12,14},{14,16},{16,18},{18... | collective-permute-start | bytes 196616 | tf_op jit(solution)/shard_map/ppermute | solution.py:49
  52.0 6.4 %collective-permute-start.15 = (f32[8,4,2,256]{3,2,1,0:T(2,128)S(1)}, f32[8,4,2,256]{3,2,1,0:T(2,128)S(1)}, u32[]{:S(2)}, u32[]{:S(2)}) collective-permute-start(f32[8,4,2,256]{3,2,1,0:T(2,128)S(1)} %get-tuple-element.32), channel_id=1, source_target_pairs={{2,0},{4,2},{6,4},{8,6},{10,8},{12,10},{14,12},{16,14},{18,16},{20... | collective-permute-start | bytes 196616 | tf_op jit(solution)/shard_map/ppermute | solution.py:50
  76.8 12.6 %all-to-all-start = ((f32[16,1,192]{2,1,0:T(1,128)}), f32[16,1,192]{2,1,0:T(1,128)S(1)}, u32[]{:S(2)}, u32[]{:S(2)}) async-start(f32[16,1,192]{2,1,0:T(1,128)} %reshape.116), calls=%async_computation | async-start | bytes 32768 | tf_op jit(solution)/shard_map/all_to_all | solution.py:128
  119.3 6.4 %collective-permute-start.16 = (f32[8,4,2,256]{3,2,1,0:T(2,128)S(1)}, f32[8,4,2,256]{3,2,1,0:T(2,128)S(1)}, u32[]{:S(2)}, u32[]{:S(2)}) collective-permute-start(f32[8,4,2,256]{3,2,1,0:T(2,128)S(1)} %get-tuple-element.29), channel_id=1, source_target_pairs={{0,2},{2,4},{4,6},{6,8},{8,10},{10,12},{12,14},{14,16},{16,18},{18... | collective-permute-start | bytes 196616 | tf_op jit(solution)/shard_map/ppermute | solution.py:49
  119.3 6.4 %collective-permute-start.17 = (f32[8,4,2,256]{3,2,1,0:T(2,128)S(1)}, f32[8,4,2,256]{3,2,1,0:T(2,128)S(1)}, u32[]{:S(2)}, u32[]{:S(2)}) collective-permute-start(f32[8,4,2,256]{3,2,1,0:T(2,128)S(1)} %get-tuple-element.30), channel_id=1, source_target_pairs={{2,0},{4,2},{6,4},{8,6},{10,8},{12,10},{14,12},{16,14},{18,16},{20... | collective-permute-start | bytes 196616 | tf_op jit(solution)/shard_map/ppermute | solution.py:50
  128.4 6.4 %collective-permute-start.18 = (f32[8,4,2,256]{3,2,1,0:T(2,128)S(1)}, f32[8,4,2,256]{3,2,1,0:T(2,128)S(1)}, u32[]{:S(2)}, u32[]{:S(2)}) collective-permute-start(f32[8,4,2,256]{3,2,1,0:T(2,128)S(1)} %get-tuple-element.27), channel_id=1, source_target_pairs={{0,2},{2,4},{4,6},{6,8},{8,10},{10,12},{12,14},{14,16},{16,18},{18... | collective-permute-start | bytes 196616 | tf_op jit(solution)/shard_map/ppermute | solution.py:49
  128.5 6.4 %collective-permute-start.19 = (f32[8,4,2,256]{3,2,1,0:T(2,128)S(1)}, f32[8,4,2,256]{3,2,1,0:T(2,128)S(1)}, u32[]{:S(2)}, u32[]{:S(2)}) collective-permute-start(f32[8,4,2,256]{3,2,1,0:T(2,128)S(1)} %get-tuple-element.28), channel_id=1, source_target_pairs={{2,0},{4,2},{6,4},{8,6},{10,8},{12,10},{14,12},{16,14},{18,16},{20... | collective-permute-start | bytes 196616 | tf_op jit(solution)/shard_map/ppermute | solution.py:50
  137.5 6.5 %collective-permute-start.20 = (f32[8,4,2,256]{3,2,1,0:T(2,128)S(1)}, f32[8,4,2,256]{3,2,1,0:T(2,128)S(1)}, u32[]{:S(2)}, u32[]{:S(2)}) collective-permute-start(f32[8,4,2,256]{3,2,1,0:T(2,128)S(1)} %get-tuple-element.25), channel_id=1, source_target_pairs={{0,2},{2,4},{4,6},{6,8},{8,10},{10,12},{12,14},{14,16},{16,18},{18... | collective-permute-start | bytes 196616 | tf_op jit(solution)/shard_map/ppermute | solution.py:49
  137.5 6.7 %collective-permute-start.21 = (f32[8,4,2,256]{3,2,1,0:T(2,128)S(1)}, f32[8,4,2,256]{3,2,1,0:T(2,128)S(1)}, u32[]{:S(2)}, u32[]{:S(2)}) collective-permute-start(f32[8,4,2,256]{3,2,1,0:T(2,128)S(1)} %get-tuple-element.26), channel_id=1, source_target_pairs={{2,0},{4,2},{6,4},{8,6},{10,8},{12,10},{14,12},{16,14},{18,16},{20... | collective-permute-start | bytes 196616 | tf_op jit(solution)/shard_map/ppermute | solution.py:50
  146.9 14.9 %collective-permute-start.22 = (f32[8,4,1,256]{3,2,1,0:T(1,128)S(1)}, f32[8,4,1,256]{3,2,1,0:T(1,128)S(1)}, u32[]{:S(2)}, u32[]{:S(2)}) collective-permute-start(f32[8,4,1,256]{3,2,1,0:T(1,128)S(1)} %get-tuple-element.23), channel_id=1, source_target_pairs={{0,2},{2,4},{4,6},{6,8},{8,10},{10,12},{12,14},{14,16},{16,18},{18... | collective-permute-start | bytes 98312 | tf_op jit(solution)/shard_map/ppermute | solution.py:49
  147.0 14.8 %collective-permute-start.23 = (f32[8,4,1,256]{3,2,1,0:T(1,128)S(1)}, f32[8,4,1,256]{3,2,1,0:T(1,128)S(1)}, u32[]{:S(2)}, u32[]{:S(2)}) collective-permute-start(f32[8,4,1,256]{3,2,1,0:T(1,128)S(1)} %get-tuple-element.24), channel_id=1, source_target_pairs={{2,0},{4,2},{6,4},{8,6},{10,8},{12,10},{14,12},{16,14},{18,16},{20... | collective-permute-start | bytes 98312 | tf_op jit(solution)/shard_map/ppermute | solution.py:50
  151.5 22.5 %collective-permute-start.30 = (bf16[1,8,4,32,256]{4,3,2,1,0:T(8,128)(2,1)S(1)}, bf16[1,8,4,32,256]{4,3,2,1,0:T(8,128)(2,1)S(1)}, u32[]{:S(2)}, u32[]{:S(2)}) collective-permute-start(bf16[1,8,4,32,256]{4,3,2,1,0:T(8,128)(2,1)S(1)} %bitcast.40), channel_id=1, source_target_pairs={{0,1},{1,0},{2,3},{3,2},{4,5},{5,4},{6,7},{7,6},{8,9},{9,8},{10,11... | collective-permute-start | bytes 1572872 | tf_op jit(solution)/shard_map/ppermute | solution.py:26
  162.5 6.2 %collective-permute-start.24 = (f32[8,4,1,256]{3,2,1,0:T(1,128)S(1)}, f32[8,4,1,256]{3,2,1,0:T(1,128)S(1)}, u32[]{:S(2)}, u32[]{:S(2)}) collective-permute-start(f32[8,4,1,256]{3,2,1,0:T(1,128)S(1)} %get-tuple-element.21), channel_id=1, source_target_pairs={{0,2},{2,4},{4,6},{6,8},{8,10},{10,12},{12,14},{14,16},{16,18},{18... | collective-permute-start | bytes 98312 | tf_op jit(solution)/shard_map/ppermute | solution.py:49
  176.5 8.1 %collective-permute-start.28 = (f32[8,4,1,256]{3,2,1,0:T(1,128)S(1)}, f32[8,4,1,256]{3,2,1,0:T(1,128)S(1)}, u32[]{:S(2)}, u32[]{:S(2)}) collective-permute-start(f32[8,4,1,256]{3,2,1,0:T(1,128)S(1)} %get-tuple-element.17), channel_id=1, source_target_pairs={{0,2},{2,4},{4,6},{6,8},{8,10},{10,12},{12,14},{14,16},{16,18},{18... | collective-permute-start | bytes 98312 | tf_op jit(solution)/shard_map/ppermute | solution.py:49
  176.5 8.0 %collective-permute-start.29 = (f32[8,4,1,256]{3,2,1,0:T(1,128)S(1)}, f32[8,4,1,256]{3,2,1,0:T(1,128)S(1)}, u32[]{:S(2)}, u32[]{:S(2)}) collective-permute-start(f32[8,4,1,256]{3,2,1,0:T(1,128)S(1)} %get-tuple-element.18), channel_id=1, source_target_pairs={{2,0},{4,2},{6,4},{8,6},{10,8},{12,10},{14,12},{16,14},{18,16},{20... | collective-permute-start | bytes 98312 | tf_op jit(solution)/shard_map/ppermute | solution.py:50
  (16 other events, 132.5 us)
